TPU v7x, 32 devices: a whole 2x2x4 slice. The times are simulated.
32 devices in a mesh: seq: 8 (over z, core), grp: 2 (over y), dp: 2 (over x).
Axes of the slice: x: 2, y: 2, z: 4, core: 2. Of those that a mesh axis runs over, the one named last changes fastest.
Arguments:
- clips: bfloat16 [2, 1024, 1408], P('dp', 'seq'), may hold values from -6 to 6
- context: int32 [2, 1024], P('dp', 'seq'), may hold values from 0 to 1, as said below
- predict_index: int32 [2, 1536], P('dp', 'seq'), may hold values from -1 to 1023, as said below
- target_qkv: bfloat16 [3, 1408, 1408], P(None, 'dp', 'grp'), may hold values from -8 to 8
- target_out: bfloat16 [1408, 1408], P('grp'), may hold values from -0.15625 to 0.15625
- student_qkv: bfloat16 [3, 1408, 1408], P(None, 'dp', 'grp'), may hold values from -8 to 8
- student_out: bfloat16 [1408, 1408], P('grp', 'dp'), may hold values from -0.15625 to 0.15625
- mask_token: float32 [1408], replicated, may hold values from -4 to 4
Outputs:
- out_grad: float32 [1408, 1408], P('grp', 'dp')
- target_blend: float32 [1408, 1408], P('grp')
Inputs may be any that keep to these rules, and one draw needn't show every extreme that they name: In every aligned block of 128 tokens of a clip exactly 32 tokens have context 1 and the others 0. `predict_index`: each device's 192 slots name distinct target positions (context 0) of its clip, followed by -1 in the unused slots; different devices' lists may name the same position. In every clip one list is full.
All inputs are finite; a program needn't handle non-finite values.
Results may differ from a plain program's by a relative error of at most 0.014.
Values may be sent and summed in bfloat16 or wider, within the bound.
A program may use at most 128 MiB of HBM per device.

v0:
```python
import math
import jax
import jax.numpy as jnp
from jax import lax
from jax.sharding import PartitionSpec as P

HEAD_DIM = 88
CTX_DEV = 32
EPSILON = 1e-06
MOMENTUM = 0.99


def layer_norm(values):
    center = values - jnp.mean(values, axis=-1, keepdims=True)
    factor = lax.rsqrt(jnp.mean(center * center, axis=-1, keepdims=True) + EPSILON)
    return (center * factor, factor)


def position_table(places, width):
    half_width = width // 2
    spacing = jnp.exp(jnp.arange(half_width, dtype=jnp.float32) * (-math.log(10000.0) / half_width))
    angles = places.astype(jnp.float32)[:, None] * spacing[None, :]
    return jnp.concatenate([jnp.sin(angles), jnp.cos(angles)], axis=1)


def to_heads(queries):
    head_count = queries.shape[1] // HEAD_DIM
    return queries.reshape(queries.shape[0], head_count, HEAD_DIM).transpose(1, 0, 2)


def empty_state(head_count, row_count):
    peaks = jnp.full((head_count, row_count), -1e30, jnp.float32)
    totals = jnp.zeros((head_count, row_count), jnp.float32)
    summed = jnp.zeros((head_count, row_count, HEAD_DIM), jnp.float32)
    return (peaks, totals, summed)


def from_heads(running):
    peaks, totals, summed = running
    mixed = summed / totals[:, :, None]
    head_count, row_count, unused = mixed.shape
    return mixed.transpose(1, 0, 2).reshape(row_count, head_count * HEAD_DIM).astype(jnp.bfloat16)


def attend_shard(running, shard_rows, query_heads):
    peaks, totals, summed = running
    key_rows, value_rows = shard_rows
    length = key_rows.shape[0]
    head_count = query_heads.shape[0]
    key_heads = key_rows.reshape(length, head_count, HEAD_DIM)
    value_heads = value_rows.reshape(length, head_count, HEAD_DIM)
    factor = HEAD_DIM ** (-0.5)
    scores = (
        jnp.einsum("hqd,khd->hqk", query_heads, key_heads, preferred_element_type=jnp.float32)
        * factor
    )
    raised = jnp.maximum(peaks, jnp.max(scores, axis=2))
    shifted = jnp.exp(scores - raised[:, :, None])
    totals = jnp.sum(shifted, axis=2)
    summed = jnp.einsum(
        "hqk,khd->hqd",
        shifted.astype(jnp.bfloat16),
        value_heads,
        preferred_element_type=jnp.float32,
    )
    return (raised, totals, summed)


def body(
    clips, context, predict_index, target_qkv, target_out, student_qkv, student_out, mask_token
):
    tokens = clips[0]
    keep_flags = context[0]
    listed = predict_index[0]
    row_count, width = tokens.shape
    half_width = target_qkv.shape[2]
    head_count = half_width // HEAD_DIM
    normed = layer_norm(tokens.astype(jnp.float32))[0].astype(jnp.bfloat16)
    projected = jnp.einsum(
        "nr,krc->knc",
        normed,
        lax.all_gather(target_qkv, "dp", axis=1, tiled=True),
        preferred_element_type=jnp.float32,
    )
    projected = projected.astype(jnp.bfloat16)
    target_state = attend_shard(
        empty_state(head_count, row_count),
        (
            lax.all_gather(projected[1], "seq", axis=0, tiled=True),
            lax.all_gather(projected[2], "seq", axis=0, tiled=True),
        ),
        query_heads=to_heads(projected[0]),
    )
    target_mixed = from_heads(target_state)
    target_part = jnp.dot(target_mixed, target_out, preferred_element_type=jnp.float32)
    target_sum = lax.psum(target_part.astype(jnp.bfloat16), "grp").astype(jnp.float32)
    features = layer_norm(tokens.astype(jnp.float32) + target_sum)[0].astype(jnp.bfloat16)
    first_row = lax.axis_index("seq") * row_count
    every_list = lax.all_gather(listed, "seq", axis=0, tiled=True)
    places = first_row + jnp.arange(row_count, dtype=jnp.int32)
    usable = jnp.sum((every_list[None, :] == places[:, None]).astype(jnp.float32), axis=1)
    slot_count = places.shape[0]
    is_context = keep_flags == 1
    context_order = jnp.cumsum(is_context.astype(jnp.int32)) - 1
    selector = (
        (context_order[None, :] == jnp.arange(CTX_DEV, dtype=jnp.int32)[:, None])
        & is_context[None, :]
    ).astype(jnp.bfloat16)
    context_rows = jnp.dot(selector, normed, preferred_element_type=jnp.float32).astype(
        jnp.bfloat16
    )
    seeds = mask_token[None, :] + position_table(jnp.maximum(places, 0), width)
    seed_normed = layer_norm(seeds)[0].astype(jnp.bfloat16)
    shard_rows = lax.all_gather(student_qkv, "dp", axis=1, tiled=True)
    query_total = jnp.dot(seed_normed, shard_rows[0], preferred_element_type=jnp.float32)
    pair_total = jnp.einsum(
        "nr,krc->knc", context_rows, shard_rows[1:], preferred_element_type=jnp.float32
    )
    student_pairs = pair_total
    student_pairs = student_pairs.astype(jnp.bfloat16)
    student_state = attend_shard(
        empty_state(head_count, slot_count),
        (
            lax.all_gather(student_pairs[0], "seq", axis=0, tiled=True),
            lax.all_gather(student_pairs[1], "seq", axis=0, tiled=True),
        ),
        query_heads=to_heads(query_total.astype(jnp.bfloat16)),
    )
    student_mixed = from_heads(student_state)
    relaid = lax.all_gather(student_out, "dp", axis=1, tiled=True)
    student_part = jnp.dot(student_mixed, relaid, preferred_element_type=jnp.float32)
    student_sum = lax.psum(student_part.astype(jnp.bfloat16), "grp").astype(jnp.float32)
    predicted, factor = layer_norm(seeds + student_sum)
    wanted = features.astype(jnp.float32)
    slope = jnp.clip(predicted - wanted, -1.0, 1.0) * usable[:, None]
    back_grad = (
        slope
        - jnp.mean(slope, axis=1, keepdims=True)
        - predicted * jnp.mean(slope * predicted, axis=1, keepdims=True)
    ) * factor
    local_grad = jnp.dot(
        student_mixed.astype(jnp.float32).T, back_grad, precision=lax.Precision.HIGHEST
    )
    column_grad = lax.psum_scatter(
        local_grad.astype(jnp.bfloat16), "dp", scatter_dimension=1, tiled=True
    )
    out_grad = lax.psum(column_grad, "seq").astype(jnp.float32)
    target_blend = MOMENTUM * target_out.astype(jnp.float32) + (1.0 - MOMENTUM) * relaid.astype(
        jnp.float32
    )
    return (out_grad, target_blend)


def solution(mesh):
    in_specs = (
        P("dp", "seq", None),
        P("dp", "seq"),
        P("dp", "seq"),
        P(None, "dp", "grp"),
        P("grp", None),
        P(None, "dp", "grp"),
        P("grp", "dp"),
        P(),
    )
    out_specs = (P("grp", "dp"), P("grp", None))
    return jax.shard_map(body, mesh=mesh, in_specs=in_specs, out_specs=out_specs, check_vma=False)
```

profile of v0, /device:TPU:0, one launch (start us, length us, event | category | flops | bytes accessed | tf_op | source)
XLA Modules:
  0.0 480.1 jit_solution(4295476264770077709)
XLA Ops:
  7.2 6.9 %copy.48 = bf16[3,704,704]{2,0,1:T(4,128)(2,1)} copy(bf16[3,704,704]{2,1,0:T(8,128)(2,1)} %param.11) | data formatting | bytes 5947392 | tf_op args[3]
  14.2 4.8 %copy.41 = bf16[3,704,704]{2,0,1:T(4,128)(2,1)} copy(bf16[3,704,704]{2,1,0:T(8,128)(2,1)S(1)} %copy-done.5) | data formatting | bytes 5947392 | tf_op args[5]
  19.1 1.2 copy-done.6
  20.3 1.5 copy.47
  21.9 0.2 fusion.45
  22.2 104.2 %all-gather.15.cloned.1.call-done = bf16[3,1408,704]{2,0,1:T(4,128)(2,1)} async-done(((bf16[3,704,704]{2,0,1:T(4,128)(2,1)}), bf16[3,1408,704]{2,0,1:T(4,128)(2,1)}) %all-gather.15.cloned.1.call-update) | async-done | bytes 5947408 | tf_op jit(solution)/shard_map/all_gather | solution.py:82
  126.4 6.0 %fusion.16 = bf16[3,128,704]{1,2,0:T(8,128)(2,1)S(1)} fusion(bf16[3,1408,704]{2,0,1:T(4,128)(2,1)} %all-gather.15.cloned.1.call-done, bf16[1,128,1408]{2,1,0:T(8,128)(2,1)S(1)} %copy-done.1, f32[128]{0:T(128)S(1)} %add_rsqrt_fusion.2, f32[128]{0:T(128)S(1)} %broadcast_multiply_fusion.4), kind=kOutput, calls=%fused_computation.21 | convolution fusion | flops 762257408 | bytes 6849536 | tf_op jit(solution)/shard_map/nr,krc->knc/dot_general | solution.py:79
  132.4 0.8 fusion.83
  133.9 1.4 multiply_sine_fusion
  135.4 0.2 fusion.66
  135.6 0.3 multiply_reduce_fusion.4
  135.9 101.4 %all-gather.11.cloned.1.call-done = bf16[3,1408,704]{2,0,1:T(4,128)(2,1)} async-done(((bf16[3,704,704]{2,0,1:T(4,128)(2,1)}), bf16[3,1408,704]{2,0,1:T(4,128)(2,1)}) %all-gather.11.cloned.1.call-update) | async-done | bytes 5947408 | tf_op jit(solution)/shard_map/all_gather | solution.py:114
  237.3 7.6 %slice.29 = bf16[2,1408,704]{2,0,1:T(2,128)(2,1)} slice(bf16[3,1408,704]{2,0,1:T(4,128)(2,1)} %all-gather.11.cloned.1.call-done), slice={[1:3], [0:1408], [0:704]} | slice | bytes 7929856 | tf_op jit(solution)/shard_map/slice | solution.py:117
  244.9 3.7 fusion.30
  248.6 0.6 fusion.84
  249.3 14.5 %all-gather.1 = bf16[1,256,704]{2,1,0:T(8,128)(2,1)S(1)} all-gather(bf16[1,32,704]{2,1,0:T(8,128)(2,1)S(1)} %get-tuple-element.19), channel_id=3, replica_groups=mesh['seq'=8,'grp'=2,'dp'=2] {'seq'}, dimensions={1}, use_global_device_ids=true | all-gather | bytes 405504 | tf_op jit(solution)/shard_map/all_gather | solution.py:125
  263.7 0.9 copy.46
  264.7 7.1 %slice.28 = bf16[1,1408,704]{2,0,1:T(2,128)(2,1)} slice(bf16[3,1408,704]{2,0,1:T(4,128)(2,1)} %all-gather.11.cloned.1.call-done), slice={[0:1], [0:1408], [0:704]} | slice | bytes 3964928 | tf_op jit(solution)/shard_map/slice | solution.py:115
  271.7 12.0 %copy.54 = bf16[1,1408,704]{1,2,0:T(8,128)(2,1)S(1)} copy(bf16[1,1408,704]{2,0,1:T(2,128)(2,1)} %slice.28) | data formatting | bytes 3964928
  283.8 16.5 %all-gather = bf16[1,256,704]{2,1,0:T(8,128)(2,1)S(1)} all-gather(bf16[1,32,704]{2,1,0:T(8,128)(2,1)} %get-tuple-element.18), channel_id=2, replica_groups=mesh['seq'=8,'grp'=2,'dp'=2] {'seq'}, dimensions={1}, use_global_device_ids=true | all-gather | bytes 405504 | tf_op jit(solution)/shard_map/all_gather | solution.py:124
  300.3 0.9 copy.45
  301.2 0.8 fusion.23
  302.0 1.4 fusion.85
  303.5 0.4 fusion.39
  303.9 0.4 fusion.26
  304.3 3.2 convolution_convert_fusion.2
  307.5 2.2 multiply_reduce_fusion
  309.7 1.9 copy-done
  311.6 0.9 fusion.4
  312.5 18.5 %all-gather.19.cloned.1.call-done = bf16[1,1024,704]{1,2,0:T(8,128)(2,1)} async-done(((bf16[1,128,704]{1,2,0:T(8,128)(2,1)}), bf16[1,1024,704]{1,2,0:T(8,128)(2,1)}) %all-gather.19.cloned.1.call-update) | async-done | bytes 1441808 | tf_op jit(solution)/shard_map/all_gather | solution.py:90
  331.0 3.6 fusion.36
  334.7 1.2 convolution_convert_fusion.1
  336.0 0.6 dynamic-slice
  337.3 0.3 dynamic-update-slice
  337.6 7.6 %all-reduce = s32[1536]{0:T(1024)S(1)} all-reduce(s32[1536]{0:T(1024)S(1)} %dynamic-update-slice), channel_id=6, replica_groups=mesh['seq'=8,'grp'=2,'dp'=2] {'seq'}, use_global_device_ids=true, to_apply=%add | all-reduce | flops 1536 | bytes 12288
  345.4 22.1 %all-reduce.7.cloned.1.call-done = (bf16[128,1408]{1,0:T(8,128)(2,1)}, bf16[128,1408]{1,0:T(8,128)(2,1)}) async-done(((bf16[128,1408]{1,0:T(8,128)(2,1)}, bf16[128,1408]{1,0:T(8,128)(2,1)}), (bf16[128,1408]{1,0:T(8,128)(2,1)}, bf16[128,1408]{1,0:T(8,128)(2,1)})) %all-reduce.7.cloned.1.call-update) | async-done | bytes 720912 | tf_op jit(solution)/shard_map/psum | solution.py:96
  367.6 1.2 fusion.53
  368.8 1.4 fusion.82
  370.5 0.5 fusion.51
  371.0 2.0 convolution_convert_fusion
  373.0 2.5 copy.52
  375.6 4.1 copy.50
  379.7 28.6 %reduce-scatter.4.cloned.1.call-done = bf16[704,704]{1,0:T(8,128)(2,1)} async-done(((bf16[1408,704]{1,0:T(8,128)(2,1)}), bf16[704,704]{1,0:T(8,128)(2,1)}) %reduce-scatter.4.cloned.1.call-update) | async-done | bytes 991248
  408.3 2.3 copy.53
  410.7 4.3 multiply_add_fusion
  415.0 5.6 %copy.51 = f32[704,1408]{1,0:T(8,128)} copy(f32[704,1408]{0,1:T(8,128)} %multiply_add_fusion) | data formatting | bytes 7929856
  420.6 49.9 %all-reduce.5.cloned.1.call-done = bf16[704,704]{1,0:T(8,128)(2,1)} async-done(((bf16[704,704]{1,0:T(8,128)(2,1)}), bf16[704,704]{1,0:T(8,128)(2,1)}) %all-reduce.5.cloned.1.call-update) | async-done | bytes 991248 | tf_op jit(solution)/shard_map/psum | solution.py:147
  470.5 2.7 convert_element_type.121
  (65 shorter events, 1.8 us)
Async XLA Ops:
  7.2 7.1 %copy-start.5 = (bf16[3,704,704]{2,1,0:T(8,128)(2,1)S(1)}, bf16[3,704,704]{2,1,0:T(8,128)(2,1)}, u32[]{:S(2)}) copy-start(bf16[3,704,704]{2,1,0:T(8,128)(2,1)} %param.13) | copy-start | bytes 8921092
  7.2 119.2 %all-gather.15.cloned.1.call-start = ((), (), s32[]{:S(2)}) async-start(), calls=%async_computation.3 | async-start | bytes 12976128 | tf_op jit(solution)/shard_map/all_gather | solution.py:82
  14.2 223.2 %all-gather.11.cloned.1.call-start = ((), (), s32[]{:S(2)}) async-start(), calls=%async_computation.1 | async-start | bytes 12976128 | tf_op jit(solution)/shard_map/all_gather | solution.py:114
  19.0 1.2 copy-start.6
  19.0 2.8 copy-start.1
  19.1 285.2 %all-gather.13.cloned.1.call-start = ((), (), s32[]{:S(2)}) async-start(), calls=%async_computation.2 | async-start | bytes 3244032 | tf_op jit(solution)/shard_map/all_gather | solution.py:130
  21.8 285.7 %all-gather.17.cloned.1.call-start = ((), (), s32[]{:S(2)}) async-start(), calls=%async_computation.5 | async-start | bytes 1622016 | tf_op jit(solution)/shard_map/all_gather | solution.py:89
  22.2 111.3 %copy-start.11 = (s32[1,128]{1,0:T(1,128)S(1)}, s32[1,128]{1,0:T(1,128)}, u32[]{:S(2)}) copy-start(s32[1,128]{1,0:T(1,128)} %param.9) | copy-start | bytes 1540
  22.2 113.1 %copy-start.9 = (f32[1408]{0:T(1024)S(1)}, f32[1408]{0:T(1024)}, u32[]{:S(2)}) copy-start(f32[1408]{0:T(1024)} %param.15) | copy-start | bytes 16900
  133.2 197.8 %all-gather.19.cloned.1.call-start = ((), (), s32[]{:S(2)}) async-start(), calls=%async_computation.6 | async-start | bytes 1622016 | tf_op jit(solution)/shard_map/all_gather | solution.py:90
  283.8 83.8 %all-reduce.7.cloned.1.call-start = ((), (), s32[]{:S(2)}) async-start(), calls=%async_computation.8 | async-start | bytes 1441792 | tf_op jit(solution)/shard_map/psum | solution.py:96
  301.2 2.6 copy-start.8
  302.0 5.5 %copy-start.7 = (bf16[1,128,704]{1,2,0:T(8,128)(2,1)S(1)}, bf16[1,128,704]{1,2,0:T(8,128)(2,1)}, u32[]{:S(2)}) copy-start(bf16[1,128,704]{1,2,0:T(8,128)(2,1)} %get-tuple-element.17) | copy-start | bytes 540676
  309.7 1.9 copy-start
  312.5 22.2 %copy-start.3 = (bf16[704,1408]{1,0:T(8,128)(2,1)S(1)}, bf16[704,1408]{1,0:T(8,128)(2,1)}, u32[]{:S(2)}) copy-start(bf16[704,1408]{1,0:T(8,128)(2,1)} %param.12) | copy-start | bytes 5947396
  331.0 5.0 %copy-start.12 = (u32[32]{0:T(128)S(1)}, u32[32]{0:T(128)}, u32[]{:S(2)}) copy-start(u32[32]{0:T(128)} %constant.55) | copy-start | bytes 388
  331.0 6.3 %copy-start.10 = (s32[1,192]{1,0:T(1,128)S(1)}, s32[1,192]{1,0:T(1,128)}, u32[]{:S(2)}) copy-start(s32[1,192]{1,0:T(1,128)} %param.10) | copy-start | bytes 2308
  336.0 72.4 %reduce-scatter.4.cloned.1.call-start = ((), (), s32[]{:S(2)}) async-start(), calls=%async_computation.7 | async-start | bytes 3244032
  367.6 2.9 copy-start.4
  375.5 35.1 %copy-start.2 = (bf16[704,1408]{0,1:T(8,128)(2,1)S(1)}, bf16[704,1408]{0,1:T(8,128)(2,1)}, u32[]{:S(2)}) copy-start(bf16[704,1408]{0,1:T(8,128)(2,1)} %all-gather.13.cloned.1.call-done) | copy-start | bytes 5947396
  375.5 95.0 %all-reduce.5.cloned.1.call-start = ((), (), s32[]{:S(2)}) async-start(), calls=%async_computation.4 | async-start | bytes 2162688 | tf_op jit(solution)/shard_map/psum | solution.py:147
Sparse Core Ops, SparseCore 0:
  14.3 112.0 all-gather.14
  128.0 109.3 all-gather.10
  239.5 33.8 all-gather.12
  274.8 28.2 all-gather.16
  304.5 26.4 all-gather.18
  336.1 31.4 all-reduce.6
  375.7 32.6 reduce-scatter.3
  411.2 59.2 all-reduce.4
where the time goes:
time: 481 us; the launch traced here: 480 us
  waiting for transfers between devices  325 us (68%)
  local copies, waits for them, and re-layouts  61.8 us (13%)
  blocking collectives  38.6 us (8%)
  matrix products  24.5 us (5%)
  between operations  15.1 us (3%)
  other arithmetic  14.7 us (3%)
    all_gather x1, waiting for transfers between devices, body(): lax.all_gather(target_qkv, 'dp', axis=1, tiled=True)  104 us
    all_gather x1, waiting for transfers between devices, body(): shard_rows = lax.all_gather(student_qkv, 'dp', axis=1, tiled=True)  101 us
    psum x1, waiting for transfers between devices, body(): out_grad = lax.psum(column_grad, 'seq').astype(jnp.float32)  49.9 us
    unnamed x37, local copies, waits for them, and re-layouts  43.8 us
    unnamed x9, waiting for transfers between devices  28.7 us
    psum x1, waiting for transfers between devices, body(): lax.psum(target_part.astype(jnp.bfloat16), 'grp').astype(jnp.float32)  22.1 us
    all_gather x1, waiting for transfers between devices, body(): lax.all_gather(projected[2], 'seq', axis=0, tiled=True)  18.5 us
    all_gather x1, blocking collectives, body(): lax.all_gather(student_pairs[0], 'seq', axis=0, tiled=True)  16.5 us
  transfers between devices with their start and end apart: 8, of which 6 were waited for; matrix products, arithmetic and copies ran while one was open for 15% of the time, Pallas kernels for 0%

commit v1 on v0

--- a/solution.py
+++ b/solution.py
@@ -79,7 +79,7 @@
     projected = jnp.einsum(
         "nr,krc->knc",
         normed,
-        lax.all_gather(target_qkv, "dp", axis=1, tiled=True),
+        jnp.concatenate(lax.all_gather(target_qkv, "dp"), axis=1),
         preferred_element_type=jnp.float32,
     )
     projected = projected.astype(jnp.bfloat16)

time: 481 us -> 450 us (0.936)
  waiting for transfers between devices: 325 us -> 268 us
  local copies, waits for them, and re-layouts: 61.8 us -> 88.8 us
    all_gather x1, waiting for transfers between devices: 101 us -> 70.4 us  [body(): shard_rows = lax.all_gather(student_qkv, 'dp', axis=1, tiled=True)]
    all_gather x1, waiting for transfers between devices: 104 us -> 77.7 us  [body(): lax.all_gather(target_qkv, 'dp')]
    all_gather x0 -> x1, local copies, waits for them, and re-layouts: none -> 18.4 us  [body(): lax.all_gather(target_qkv, 'dp')]
    reshape x0 -> x1, local copies, waits for them, and re-layouts: none -> 14.3 us  [body(): jnp.concatenate(lax.all_gather(target_qkv, 'dp'), axis=1)]
    unnamed x37 -> x36, local copies, waits for them, and re-layouts: 43.8 us -> 38.1 us
  transfers between devices with their start and end apart: 8 -> 8, of which waited for: 6 -> 6; matrix products, arithmetic and copies ran while one was open for 15% -> 23% of each run, Pallas kernels for 0% -> 0%
where the time goes in v1:
time: 450 us; the launch traced here: 449 us
  waiting for transfers between devices  268 us (60%)
  local copies, waits for them, and re-layouts  88.8 us (20%)
  blocking collectives  38.7 us (9%)
  matrix products  23 us (5%)
  between operations  15 us (3%)
  other arithmetic  14.7 us (3%)
    all_gather x1, waiting for transfers between devices, body(): lax.all_gather(target_qkv, 'dp')  77.7 us
    all_gather x1, waiting for transfers between devices, body(): shard_rows = lax.all_gather(student_qkv, 'dp', axis=1, tiled=True)  70.4 us
    psum x1, waiting for transfers between devices, body(): out_grad = lax.psum(column_grad, 'seq').astype(jnp.float32)  49.9 us
    unnamed x36, local copies, waits for them, and re-layouts  38.1 us
    unnamed x9, waiting for transfers between devices  29.4 us
    psum x1, waiting for transfers between devices, body(): lax.psum(target_part.astype(jnp.bfloat16), 'grp').astype(jnp.float32)  22.1 us
    all_gather x1, waiting for transfers between devices, body(): lax.all_gather(projected[2], 'seq', axis=0, tiled=True)  18.5 us
    all_gather x1, local copies, waits for them, and re-layouts, body(): lax.all_gather(target_qkv, 'dp')  18.4 us
  transfers between devices with their start and end apart: 8, of which 6 were waited for; matrix products, arithmetic and copies ran while one was open for 23% of the time, Pallas kernels for 0%

profile of v1, /device:TPU:0, one launch (start us, length us, event | category | flops | bytes accessed | tf_op | source)
XLA Modules:
  0.0 448.7 jit_solution(6439592363940196900)
XLA Ops:
  7.2 0.7 all-gather.16.cloned.1.call-update
  8.0 1.1 copy-done.5
  9.1 4.8 %copy.39 = bf16[3,704,704]{2,0,1:T(4,128)(2,1)} copy(bf16[3,704,704]{2,1,0:T(8,128)(2,1)S(1)} %copy-done.5) | data formatting | bytes 5947392 | tf_op args[5]
  14.0 1.2 copy-done.6
  15.2 1.5 copy.45
  17.1 77.7 %all-gather.16.cloned.1.call-done = bf16[6,704,704]{2,1,0:T(8,128)(2,1)} async-done(((bf16[3,704,704]{2,1,0:T(8,128)(2,1)}), bf16[6,704,704]{2,1,0:T(8,128)(2,1)}) %all-gather.16.cloned.1.call-update) | async-done | bytes 5947408 | tf_op jit(solution)/shard_map/all_gather | solution.py:82
  94.8 18.4 %copy.46 = bf16[2,3,704,704]{2,0,3,1:T(2,128)(2,1)} copy(bf16[2,3,704,704]{3,2,1,0:T(8,128)(2,1)} %bitcast.94) | data formatting | bytes 11894784 | tf_op jit(solution)/shard_map/all_gather | solution.py:82
  113.3 14.3 %reshape.161 = bf16[3,1408,704]{1,2,0:T(8,128)(2,1)} reshape(bf16[3,2,704,704]{2,1,3,0:T(2,128)(2,1)} %bitcast.92) | data formatting | bytes 11894784 | tf_op jit(solution)/shard_map/reshape | solution.py:82
  127.6 4.5 %fusion.11 = bf16[3,128,704]{1,2,0:T(8,128)(2,1)S(1)} fusion(bf16[3,1408,704]{1,2,0:T(8,128)(2,1)} %reshape.161, bf16[1,128,1408]{2,1,0:T(8,128)(2,1)S(1)} %copy-done.1, f32[128]{0:T(128)S(1)} %add_rsqrt_fusion.2, f32[128]{0:T(128)S(1)} %broadcast_multiply_fusion.4), kind=kOutput, calls=%fused_computation.19 | convolution fusion | flops 762257408 | bytes 6849536 | tf_op jit(solution)/shard_map/nr,krc->knc/dot_general | solution.py:79
  132.1 0.8 fusion.84
  133.4 1.4 multiply_sine_fusion
  135.1 0.3 multiply_reduce_fusion.4
  135.4 70.4 %all-gather.12.cloned.1.call-done = bf16[3,1408,704]{2,0,1:T(4,128)(2,1)} async-done(((bf16[3,704,704]{2,0,1:T(4,128)(2,1)}), bf16[3,1408,704]{2,0,1:T(4,128)(2,1)}) %all-gather.12.cloned.1.call-update) | async-done | bytes 5947408 | tf_op jit(solution)/shard_map/all_gather | solution.py:114
  205.8 7.6 %slice.29 = bf16[2,1408,704]{2,0,1:T(2,128)(2,1)} slice(bf16[3,1408,704]{2,0,1:T(4,128)(2,1)} %all-gather.12.cloned.1.call-done), slice={[1:3], [0:1408], [0:704]} | slice | bytes 7929856 | tf_op jit(solution)/shard_map/slice | solution.py:117
  213.4 3.7 fusion.23
  217.1 0.6 fusion.85
  217.7 14.6 %all-gather.1 = bf16[1,256,704]{2,1,0:T(8,128)(2,1)S(1)} all-gather(bf16[1,32,704]{2,1,0:T(8,128)(2,1)S(1)} %get-tuple-element.19), channel_id=3, replica_groups=mesh['seq'=8,'grp'=2,'dp'=2] {'seq'}, dimensions={1}, use_global_device_ids=true | all-gather | bytes 405504 | tf_op jit(solution)/shard_map/all_gather | solution.py:125
  232.4 0.9 copy.44
  233.3 7.1 %slice.28 = bf16[1,1408,704]{2,0,1:T(2,128)(2,1)} slice(bf16[3,1408,704]{2,0,1:T(4,128)(2,1)} %all-gather.12.cloned.1.call-done), slice={[0:1], [0:1408], [0:704]} | slice | bytes 3964928 | tf_op jit(solution)/shard_map/slice | solution.py:115
  240.3 12.0 %copy.51 = bf16[1,1408,704]{1,2,0:T(8,128)(2,1)S(1)} copy(bf16[1,1408,704]{2,0,1:T(2,128)(2,1)} %slice.28) | data formatting | bytes 3964928
  252.4 16.4 %all-gather = bf16[1,256,704]{2,1,0:T(8,128)(2,1)S(1)} all-gather(bf16[1,32,704]{2,1,0:T(8,128)(2,1)} %get-tuple-element.18), channel_id=2, replica_groups=mesh['seq'=8,'grp'=2,'dp'=2] {'seq'}, dimensions={1}, use_global_device_ids=true | all-gather | bytes 405504 | tf_op jit(solution)/shard_map/all_gather | solution.py:124
  268.8 0.9 copy.43
  269.7 0.8 fusion.16
  270.5 1.4 fusion.86
  272.0 0.4 fusion.32
  272.4 0.4 fusion.19
  272.8 3.2 convolution_convert_fusion.2
  276.0 2.2 multiply_reduce_fusion
  278.2 1.9 copy-done
  280.1 0.9 fusion.2
  281.0 18.5 %all-gather.20.cloned.1.call-done = bf16[1,1024,704]{1,2,0:T(8,128)(2,1)} async-done(((bf16[1,128,704]{1,2,0:T(8,128)(2,1)}), bf16[1,1024,704]{1,2,0:T(8,128)(2,1)}) %all-gather.20.cloned.1.call-update) | async-done | bytes 1441808 | tf_op jit(solution)/shard_map/all_gather | solution.py:90
  299.6 3.6 fusion.29
  303.2 1.2 convolution_convert_fusion.1
  304.6 0.6 dynamic-slice
  306.1 7.6 %all-reduce = s32[1536]{0:T(1024)S(1)} all-reduce(s32[1536]{0:T(1024)S(1)} %dynamic-update-slice), channel_id=7, replica_groups=mesh['seq'=8,'grp'=2,'dp'=2] {'seq'}, use_global_device_ids=true, to_apply=%add | all-reduce | flops 1536 | bytes 12288
  314.0 22.1 %all-reduce.7.cloned.1.call-done = (bf16[128,1408]{1,0:T(8,128)(2,1)}, bf16[128,1408]{1,0:T(8,128)(2,1)}) async-done(((bf16[128,1408]{1,0:T(8,128)(2,1)}, bf16[128,1408]{1,0:T(8,128)(2,1)}), (bf16[128,1408]{1,0:T(8,128)(2,1)}, bf16[128,1408]{1,0:T(8,128)(2,1)})) %all-reduce.7.cloned.1.call-update) | async-done | bytes 720912 | tf_op jit(solution)/shard_map/psum | solution.py:96
  336.1 1.2 fusion.48
  337.4 1.4 fusion.83
  339.1 0.5 fusion.46
  339.6 2.0 convolution_convert_fusion
  341.6 2.5 copy.49
  344.2 4.1 copy.47
  348.3 28.6 %reduce-scatter.4.cloned.1.call-done = bf16[704,704]{1,0:T(8,128)(2,1)} async-done(((bf16[1408,704]{1,0:T(8,128)(2,1)}), bf16[704,704]{1,0:T(8,128)(2,1)}) %reduce-scatter.4.cloned.1.call-update) | async-done | bytes 991248
  376.9 2.3 copy.50
  379.2 4.3 multiply_add_fusion
  383.6 5.6 %copy.48 = f32[704,1408]{1,0:T(8,128)} copy(f32[704,1408]{0,1:T(8,128)} %multiply_add_fusion) | data formatting | bytes 7929856
  389.2 49.9 %all-reduce.5.cloned.1.call-done = bf16[704,704]{1,0:T(8,128)(2,1)} async-done(((bf16[704,704]{1,0:T(8,128)(2,1)}), bf16[704,704]{1,0:T(8,128)(2,1)}) %all-reduce.5.cloned.1.call-update) | async-done | bytes 991248 | tf_op jit(solution)/shard_map/psum | solution.py:147
  439.1 2.7 convert_element_type.129
  (66 shorter events, 2.4 us)
Async XLA Ops:
  7.2 1.9 copy-start.5
  7.2 87.7 %all-gather.16.cloned.1.call-start = ((), (), s32[]{:S(2)}) async-start(), calls=%async_computation.4 | async-start | bytes 9732096 | tf_op jit(solution)/shard_map/all_gather | solution.py:82
  7.9 197.9 %all-gather.12.cloned.1.call-start = ((), (), s32[]{:S(2)}) async-start(), calls=%async_computation.1 | async-start | bytes 12976128 | tf_op jit(solution)/shard_map/all_gather | solution.py:114
  13.9 1.2 copy-start.6
  13.9 2.8 copy-start.1
  14.0 258.8 %all-gather.14.cloned.1.call-start = ((), (), s32[]{:S(2)}) async-start(), calls=%async_computation.2 | async-start | bytes 3244032 | tf_op jit(solution)/shard_map/all_gather | solution.py:130
  16.7 259.3 %all-gather.18.cloned.1.call-start = ((), (), s32[]{:S(2)}) async-start(), calls=%async_computation.5 | async-start | bytes 1622016 | tf_op jit(solution)/shard_map/all_gather | solution.py:89
  127.6 5.4 %copy-start.11 = (s32[1,128]{1,0:T(1,128)S(1)}, s32[1,128]{1,0:T(1,128)}, u32[]{:S(2)}) copy-start(s32[1,128]{1,0:T(1,128)} %param.9) | copy-start | bytes 1540
  127.6 7.3 %copy-start.9 = (f32[1408]{0:T(1024)S(1)}, f32[1408]{0:T(1024)}, u32[]{:S(2)}) copy-start(f32[1408]{0:T(1024)} %param.15) | copy-start | bytes 16900
  132.9 166.7 %all-gather.20.cloned.1.call-start = ((), (), s32[]{:S(2)}) async-start(), calls=%async_computation.6 | async-start | bytes 1622016 | tf_op jit(solution)/shard_map/all_gather | solution.py:90
  252.4 83.8 %all-reduce.7.cloned.1.call-start = ((), (), s32[]{:S(2)}) async-start(), calls=%async_computation.8 | async-start | bytes 1441792 | tf_op jit(solution)/shard_map/psum | solution.py:96
  269.7 2.6 copy-start.8
  270.5 5.5 %copy-start.7 = (bf16[1,128,704]{1,2,0:T(8,128)(2,1)S(1)}, bf16[1,128,704]{1,2,0:T(8,128)(2,1)}, u32[]{:S(2)}) copy-start(bf16[1,128,704]{1,2,0:T(8,128)(2,1)} %get-tuple-element.17) | copy-start | bytes 540676
  278.2 1.9 copy-start
  281.0 22.2 %copy-start.3 = (bf16[704,1408]{1,0:T(8,128)(2,1)S(1)}, bf16[704,1408]{1,0:T(8,128)(2,1)}, u32[]{:S(2)}) copy-start(bf16[704,1408]{1,0:T(8,128)(2,1)} %param.12) | copy-start | bytes 5947396
  299.6 5.0 %copy-start.12 = (u32[32]{0:T(128)S(1)}, u32[32]{0:T(128)}, u32[]{:S(2)}) copy-start(u32[32]{0:T(128)} %constant.55) | copy-start | bytes 388
  299.6 6.3 %copy-start.10 = (s32[1,192]{1,0:T(1,128)S(1)}, s32[1,192]{1,0:T(1,128)}, u32[]{:S(2)}) copy-start(s32[1,192]{1,0:T(1,128)} %param.10) | copy-start | bytes 2308
  304.5 72.4 %reduce-scatter.4.cloned.1.call-start = ((), (), s32[]{:S(2)}) async-start(), calls=%async_computation.7 | async-start | bytes 3244032
  336.1 2.9 copy-start.4
  344.1 35.1 %copy-start.2 = (bf16[704,1408]{0,1:T(8,128)(2,1)S(1)}, bf16[704,1408]{0,1:T(8,128)(2,1)}, u32[]{:S(2)}) copy-start(bf16[704,1408]{0,1:T(8,128)(2,1)} %all-gather.14.cloned.1.call-done) | copy-start | bytes 5947396
  344.1 95.0 %all-reduce.5.cloned.1.call-start = ((), (), s32[]{:S(2)}) async-start(), calls=%async_computation.3 | async-start | bytes 2162688 | tf_op jit(solution)/shard_map/psum | solution.py:147
Sparse Core Ops, SparseCore 0:
  9.5 85.2 all-gather.15
  96.4 109.3 all-gather.11
  207.9 33.8 all-gather.13
  243.2 28.2 all-gather.17
  273.0 26.5 all-gather.19
  304.6 31.4 all-reduce.6
  344.2 32.6 reduce-scatter.3
  379.8 59.2 all-reduce.4
